TPU v7x, 128 devices: a whole 4x4x4 slice. The times are simulated.
128 devices in a mesh: row: 8 (over y, x_lo), col: 16 (over z, x_hi, core).
Axes of the slice: x: 4 (x_hi: 2, x_lo: 2; x = x_hi * 2 + x_lo), y: 4, z: 4, core: 2. Of those that a mesh axis runs over, the one named last changes fastest.
Arguments:
- teacher_feats: bfloat16 [64, 128, 4096], P(None, 'row', 'col'), may hold values from -6 to 6
- teacher_probs: float32 [8, 128, 4096], P(None, 'row', 'col'), may hold values from 0 to 1, as said below
- student_feats: bfloat16 [256, 128, 4096], P(None, 'row', 'col'), may hold values from 0 to 8
- conv_weight: bfloat16 [9, 256, 256], replicated, may hold values from -0.125 to 0.125
- class_weight: bfloat16 [256, 8], replicated, may hold values from -3 to 3
Outputs:
- refined: float32 [8, 128, 4096], P(None, 'row', 'col')
- feature_grad: bfloat16 [256, 128, 4096], P(None, 'row', 'col')
- grad_conv: float32 [9, 256, 256], replicated
- grad_class: float32 [256, 8], replicated
Inputs may be any that keep to these rules, and one draw needn't show every extreme that they name: `teacher_probs`: at every pixel the 8 values are positive and sum to one.
All inputs are finite; a program needn't handle non-finite values.
Results may differ from a plain program's by a relative error of at most 0.002.
The roundings to bfloat16 on the way count: a program that leaves them out, or rounds other values in their place, can miss the bound.
Values may be sent and summed in bfloat16 or wider, within the bound.
No kernel may reach another device: no remote copies, remote signals or barrier semaphores. Data moves between devices by JAX's collectives and lax.ppermute only.
A program may use at most 128 MiB of HBM per device.

v0:
```python
import jax
import jax.numpy as jnp
from jax import lax
from jax.sharding import PartitionSpec as P

ITERS = 4


def with_halo(cells, sides, width):
    for axis, dim in sides:
        count = lax.axis_size(axis)
        ends = count - 1
        head = lax.slice_in_dim(cells, 0, width, axis=dim)
        tail = lax.slice_in_dim(cells, cells.shape[dim] - width, cells.shape[dim], axis=dim)
        cells = jnp.concatenate(
            [
                lax.ppermute(tail, axis, [(i, (i + 1) % count) for i in range(ends)]),
                cells,
                lax.ppermute(head, axis, [((i + 1) % count, i) for i in range(ends)]),
            ],
            axis=dim,
        )
    return cells


def tap_list():
    offsets = [(0, 0)]
    for radius in (1, 2, 4):
        for step_y in (-1, 0, 1):
            for step_x in (-1, 0, 1):
                if step_y != 0 or step_x != 0:
                    offsets.append((step_y * radius, step_x * radius))
    return offsets


def conv_taps():
    return [(off_y, off_x) for off_y in (-1, 0, 1) for off_x in (-1, 0, 1)]


def window(padded, margin, off_y, off_x, rows_here, cols_here):
    return padded[
        :, margin + off_y : margin + off_y + rows_here, margin + off_x : margin + off_x + cols_here
    ]


def silu_slope(pre_act):
    logistic = jax.nn.sigmoid(pre_act)
    return logistic * (1.0 + pre_act * (1.0 - logistic))


def line_inside(start, count, extend, full):
    places = start - extend + jnp.arange(count + 2 * extend, dtype=jnp.int32)
    return ((places >= 0) & (places < full)).astype(jnp.float32)


def affinity_weights(features, inside, extend, rows_here, cols_here):
    margin = 4
    span_y = rows_here + 2 * extend
    span_x = cols_here + 2 * extend
    center = features[:, margin : margin + span_y, margin : margin + span_x].astype(jnp.float32)
    tap_terms = []
    for position, (off_y, off_x) in enumerate(tap_list()):
        if position == 0:
            tap_terms.append(jnp.ones((span_y, span_x), jnp.float32))
        else:
            neighbour = features[
                :,
                margin + off_y : margin + off_y + span_y,
                margin + off_x : margin + off_x + span_x,
            ].astype(jnp.float32)
            distance = jnp.sum((center - neighbour) ** 2, axis=0)
            present = inside[
                margin + off_y : margin + off_y + span_y, margin + off_x : margin + off_x + span_x
            ]
            tap_terms.append(present * jnp.exp(-distance / features.shape[0]))
    stacked = jnp.stack(tap_terms)
    return stacked / jnp.sum(stacked, axis=0)


def propagate(weights, padded, span_y, span_x):
    running = jnp.zeros((padded.shape[0], span_y, span_x), jnp.float32)
    for position, (off_y, off_x) in enumerate(tap_list()):
        running = running + weights[position][None] * window(
            padded, 4, off_y, off_x, span_y, span_x
        )
    return running


def shards(teacher_feats, teacher_probs, student_feats, conv_weight, class_weight):
    rows_here, cols_here = (teacher_probs.shape[1], teacher_probs.shape[2])
    row_start = lax.axis_index("row") * rows_here
    col_start = lax.axis_index("col") * cols_here
    full_rows = rows_here * lax.axis_size("row")
    full_cols = cols_here * lax.axis_size("col")
    features = with_halo(teacher_feats, (("row", 1), ("col", 2)), 4)
    inside = (
        line_inside(row_start, rows_here, 4, full_rows)[:, None]
        * line_inside(col_start, cols_here, 4, full_cols)[None, :]
    )
    weights = affinity_weights(features, inside, 0, rows_here, cols_here)
    current = teacher_probs
    for sweep_index in range(ITERS):
        padded = with_halo(current, (("row", 1), ("col", 2)), 4)
        current = propagate(weights, padded, rows_here, cols_here)
    channels = student_feats.shape[0]
    pixels = rows_here * cols_here
    pixel_count = float(rows_here * cols_here)
    student_pad = with_halo(student_feats, (("row", 1), ("col", 2)), 1)
    pre_act = jnp.zeros((conv_weight.shape[2], pixels), jnp.float32)
    for tap_index, (off_y, off_x) in enumerate(conv_taps()):
        shifted = window(student_pad, 1, off_y, off_x, rows_here, cols_here).reshape(
            channels, pixels
        )
        pre_act = pre_act + jnp.einsum(
            "ch,cp->hp", conv_weight[tap_index], shifted, preferred_element_type=jnp.float32
        )
    hidden = jax.nn.silu(pre_act).astype(jnp.bfloat16)
    class_logit = jnp.einsum("hk,hp->kp", class_weight, hidden, preferred_element_type=jnp.float32)
    error_term = (jax.nn.sigmoid(class_logit) - current.reshape(-1, pixels)).astype(jnp.bfloat16)
    back_sum = jnp.einsum("hk,kp->hp", class_weight, error_term, preferred_element_type=jnp.float32)
    back_error = (back_sum * silu_slope(pre_act)).astype(jnp.bfloat16)
    class_part = jnp.einsum("hp,kp->hk", hidden, error_term, preferred_element_type=jnp.float32)
    error_pad = with_halo(back_error.reshape(-1, rows_here, cols_here), (("row", 1), ("col", 2)), 1)
    conv_parts = []
    feature_sum = jnp.zeros((channels, pixels), jnp.float32)
    for tap_index, (off_y, off_x) in enumerate(conv_taps()):
        shifted = window(student_pad, 1, off_y, off_x, rows_here, cols_here).reshape(
            channels, pixels
        )
        tap_part = jnp.einsum("cp,hp->ch", shifted, back_error, preferred_element_type=jnp.float32)
        conv_parts.append(tap_part)
        moved = window(error_pad, 1, -off_y, -off_x, rows_here, cols_here).reshape(-1, pixels)
        feature_sum = feature_sum + jnp.einsum(
            "ch,hp->cp", conv_weight[tap_index], moved, preferred_element_type=jnp.float32
        )
    feature_grad = feature_sum.astype(jnp.bfloat16).reshape(channels, rows_here, cols_here)
    summed_conv, summed_class = lax.psum((jnp.stack(conv_parts), class_part), ("row", "col"))
    grad_conv = summed_conv / pixel_count
    grad_class = summed_class / pixel_count
    return (current, feature_grad, grad_conv, grad_class)


def solution(mesh):
    in_specs = (P(None, "row", "col"), P(None, "row", "col"), P(None, "row", "col"), P(), P())
    out_specs = (P(None, "row", "col"), P(None, "row", "col"), P(), P())
    return jax.shard_map(shards, mesh=mesh, in_specs=in_specs, out_specs=out_specs, check_vma=False)
```

profile of v0, /device:TPU:1, one launch (start us, length us, event | category | flops | bytes accessed | tf_op | source)
XLA Modules:
  0.0 411.8 jit_solution(18215868631557086135)
XLA Ops:
  9.6 4.6 %collective-permute-start.4 = (f32[8,4,256]{2,1,0:T(4,128)S(1)}, f32[8,4,256]{2,1,0:T(4,128)S(1)}, u32[]{:S(2)}, u32[]{:S(2)}) collective-permute-start(f32[8,4,256]{2,1,0:T(4,128)S(1)} %get-tuple-element.128), channel_id=1, source_target_pairs={{0,16},{16,32},{32,48},{48,64},{64,80},{80,96},{96,112},{1,17},{17... | collective-permute-start | bytes 98312 | tf_op jit(solution)/shard_map/ppermute | solution.py:17
  16.0 4.3 %collective-permute-start = (bf16[64,4,256]{2,1,0:T(4,128)(2,1)}, bf16[64,4,256]{2,1,0:T(4,128)(2,1)S(1)}, u32[]{:S(2)}, u32[]{:S(2)}) collective-permute-start(bf16[64,4,256]{2,1,0:T(4,128)(2,1)} %get-tuple-element.78), channel_id=1, source_target_pairs={{0,16},{16,32},{32,48},{48,64},{64,80},{80,96},{96,112},{1,17},{17... | collective-permute-start | bytes 393224 | tf_op jit(solution)/shard_map/ppermute | solution.py:17
  32.9 5.8 %collective-permute-start.6 = (f32[8,24,4]{2,1,0:T(8,128)S(1)}, f32[8,24,4]{2,1,0:T(8,128)S(1)}, u32[]{:S(2)}, u32[]{:S(2)}) collective-permute-start(f32[8,24,4]{2,1,0:T(8,128)S(1)} %get-tuple-element.119), channel_id=1, source_target_pairs={{0,1},{1,2},{2,3},{3,4},{4,5},{5,6},{6,7},{7,8},{8,9},{9,10},{10,1... | collective-permute-start | bytes 9224 | tf_op jit(solution)/shard_map/ppermute | solution.py:17
  40.6 5.0 %collective-permute-start.20 = (bf16[256,1,256]{2,0,1:T(8,128)(2,1)}, bf16[256,1,256]{2,0,1:T(8,128)(2,1)}, u32[]{:S(2)}, u32[]{:S(2)}) collective-permute-start(bf16[256,1,256]{2,0,1:T(8,128)(2,1)} %copy.38), channel_id=1, source_target_pairs={{0,16},{16,32},{32,48},{48,64},{64,80},{80,96},{96,112},{1,17},{17... | collective-permute-start | bytes 393224 | tf_op jit(solution)/shard_map/ppermute | solution.py:17
  51.6 5.8 %collective-permute-start.2 = (bf16[64,24,4]{2,1,0:T(8,128)(2,1)}, bf16[64,24,4]{2,1,0:T(8,128)(2,1)}, u32[]{:S(2)}, u32[]{:S(2)}) collective-permute-start(bf16[64,24,4]{2,1,0:T(8,128)(2,1)} %get-tuple-element.77), channel_id=1, source_target_pairs={{0,1},{1,2},{2,3},{3,4},{4,5},{5,6},{6,7},{7,8},{8,9},{9,10},{10,1... | collective-permute-start | bytes 36872 | tf_op jit(solution)/shard_map/ppermute | solution.py:17
  76.9 3.4 fusion.250
  83.1 3.7 pad_maximum_fusion.6
  89.6 4.3 %fusion.71 = (f32[16,256]{1,0:T(8,128)S(1)}, f32[16,256]{1,0:T(8,128)S(1)}, f32[16,256]{1,0:T(8,128)S(1)}, f32[16,256]{1,0:T(8,128)S(1)}, f32[16,256]{1,0:T(8,12...) fusion(bf16[64,16,256]{2,1,0:T(8,128)(2,1)S(1)} %copy-done.4, ...), kind=kLoop, calls=%fused_computation.134 | loop fusion | flops 18288640 | bytes 7192576 | tf_op jit(solution)/shard_map/reduce_sum | solution.py:71
  96.4 3.6 collective-permute-start.8
  102.1 4.6 %collective-permute-done.9 = f32[8,4,256]{2,1,0:T(4,128)S(1)} collective-permute-done((f32[8,4,256]{2,1,0:T(4,128)S(1)}, f32[8,4,256]{2,1,0:T(4,128)S(1)}, u32[]{:S(2)}, u32[]{:S(2)}) %collective-permute-start.9) | collective-permute-done | bytes 32800 | tf_op jit(solution)/shard_map/ppermute | solution.py:19
  106.8 7.2 %collective-permute-start.10 = (f32[8,24,4]{2,1,0:T(8,128)S(1)}, f32[8,24,4]{2,1,0:T(8,128)S(1)}, u32[]{:S(2)}, u32[]{:S(2)}) collective-permute-start(f32[8,24,4]{2,1,0:T(8,128)S(1)} %get-tuple-element.115), channel_id=1, source_target_pairs={{0,1},{1,2},{2,3},{3,4},{4,5},{5,6},{6,7},{7,8},{8,9},{9,10},{10,1... | collective-permute-start | bytes 9224 | tf_op jit(solution)/shard_map/ppermute | solution.py:17
  117.2 4.2 %collective-permute-done.11 = f32[8,24,4]{2,1,0:T(8,128)S(1)} collective-permute-done((f32[8,24,4]{2,1,0:T(8,128)S(1)}, f32[8,24,4]{2,1,0:T(8,128)S(1)}, u32[]{:S(2)}, u32[]{:S(2)}) %collective-permute-start.11) | collective-permute-done | bytes 3104 | tf_op jit(solution)/shard_map/ppermute | solution.py:19
  122.3 3.9 collective-permute-start.12
  131.0 4.0 collective-permute-start.14
  137.7 5.8 %collective-permute-done.15 = f32[8,24,4]{2,1,0:T(8,128)S(1)} collective-permute-done((f32[8,24,4]{2,1,0:T(8,128)S(1)}, f32[8,24,4]{2,1,0:T(8,128)S(1)}, u32[]{:S(2)}, u32[]{:S(2)}) %collective-permute-start.15) | collective-permute-done | bytes 3104 | tf_op jit(solution)/shard_map/ppermute | solution.py:19
  152.0 3.3 collective-permute-start.18
  158.5 4.8 %collective-permute-done.19 = f32[8,24,4]{2,1,0:T(8,128)S(1)} collective-permute-done((f32[8,24,4]{2,1,0:T(8,128)S(1)}, f32[8,24,4]{2,1,0:T(8,128)S(1)}, u32[]{:S(2)}, u32[]{:S(2)}) %collective-permute-start.19) | collective-permute-done | bytes 3104 | tf_op jit(solution)/shard_map/ppermute | solution.py:19
  167.1 69.5 %psum.15 = f32[256,8]{0,1:T(8,128)S(1)} all-reduce(f32[256,8]{0,1:T(8,128)S(1)} %fusion.264), channel_id=1, replica_groups=mesh['row'=8,'col'=16] {'row','col'}, use_global_device_ids=true, to_apply=%region_25.26 | all-reduce | flops 2048 | bytes 16384 | tf_op jit(solution)/shard_map/psum | solution.py:137
  236.6 3.2 fusion.23
  256.2 6.6 %collective-permute-done.25 = bf16[256,1,256]{0,2,1:T(8,128)(2,1)S(1)} collective-permute-done((bf16[256,1,256]{0,2,1:T(8,128)(2,1)S(1)}, bf16[256,1,256]{0,2,1:T(8,128)(2,1)S(1)}, u32[]{:S(2)}, u32[]{:S(2)}) %collective-permute-start.25) | collective-permute-done | bytes 131104 | tf_op jit(solution)/shard_map/ppermute | solution.py:19
  262.8 3.2 collective-permute-start.26
  266.0 4.2 %collective-permute-start.27 = (bf16[256,18,1]{0,2,1:T(2,128)(2,1)S(1)}, bf16[256,18,1]{0,2,1:T(2,128)(2,1)S(1)}, u32[]{:S(2)}, u32[]{:S(2)}) collective-permute-start(bf16[256,18,1]{0,2,1:T(2,128)(2,1)S(1)} %get-tuple-element.61), channel_id=1, source_target_pairs={{0,1},{1,2},{2,3},{3,4},{4,5},{5,6},{6,7},{7,8},{8,9},{9,10},{10,1... | collective-permute-start | bytes 27656 | tf_op jit(solution)/shard_map/ppermute | solution.py:17
  283.9 117.6 %all-reduce.2.cloned.1.call-done = f32[9,256,256]{2,1,0:T(8,128)} async-done(((f32[9,256,256]{2,1,0:T(8,128)}), f32[9,256,256]{2,1,0:T(8,128)}) %all-reduce.2.cloned.1.call-update) | async-done | bytes 2359312 | tf_op jit(solution)/shard_map/psum | solution.py:137
  401.5 3.3 broadcast_multiply_fusion
  (223 shorter events, 110.8 us)
Async XLA Ops:
  7.2 394.2 %all-reduce.2.cloned.1.call-start = ((), (), s32[]{:S(2)}) async-start(), calls=%async_computation | async-start | bytes 4718592 | tf_op jit(solution)/shard_map/psum | solution.py:137
  8.3 24.5 %collective-permute-start.5 = (f32[8,4,256]{2,1,0:T(4,128)S(1)}, f32[8,4,256]{2,1,0:T(4,128)S(1)}, u32[]{:S(2)}, u32[]{:S(2)}) collective-permute-start(f32[8,4,256]{2,1,0:T(4,128)S(1)} %get-tuple-element.127), channel_id=1, source_target_pairs={{16,0},{32,16},{48,32},{64,48},{80,64},{96,80},{112,96},{17,1},{33... | collective-permute-start | bytes 98312 | tf_op jit(solution)/shard_map/ppermute | solution.py:19
  9.6 23.2 %collective-permute-start.4 = (f32[8,4,256]{2,1,0:T(4,128)S(1)}, f32[8,4,256]{2,1,0:T(4,128)S(1)}, u32[]{:S(2)}, u32[]{:S(2)}) collective-permute-start(f32[8,4,256]{2,1,0:T(4,128)S(1)} %get-tuple-element.128), channel_id=1, source_target_pairs={{0,16},{16,32},{32,48},{48,64},{64,80},{80,96},{96,112},{1,17},{17... | collective-permute-start | bytes 98312 | tf_op jit(solution)/shard_map/ppermute | solution.py:17
  16.0 31.1 %collective-permute-start = (bf16[64,4,256]{2,1,0:T(4,128)(2,1)}, bf16[64,4,256]{2,1,0:T(4,128)(2,1)S(1)}, u32[]{:S(2)}, u32[]{:S(2)}) collective-permute-start(bf16[64,4,256]{2,1,0:T(4,128)(2,1)} %get-tuple-element.78), channel_id=1, source_target_pairs={{0,16},{16,32},{32,48},{48,64},{64,80},{80,96},{96,112},{1,17},{17... | collective-permute-start | bytes 393224 | tf_op jit(solution)/shard_map/ppermute | solution.py:17
  20.3 26.9 %collective-permute-start.1 = (bf16[64,4,256]{2,1,0:T(4,128)(2,1)}, bf16[64,4,256]{2,1,0:T(4,128)(2,1)}, u32[]{:S(2)}, u32[]{:S(2)}) collective-permute-start(bf16[64,4,256]{2,1,0:T(4,128)(2,1)} %get-tuple-element.79), channel_id=1, source_target_pairs={{16,0},{32,16},{48,32},{64,48},{80,64},{96,80},{112,96},{17,1},{33... | collective-permute-start | bytes 393224 | tf_op jit(solution)/shard_map/ppermute | solution.py:19
  24.2 33.2 %collective-permute-start.21 = (bf16[256,1,256]{2,0,1:T(8,128)(2,1)}, bf16[256,1,256]{2,0,1:T(8,128)(2,1)}, u32[]{:S(2)}, u32[]{:S(2)}) collective-permute-start(bf16[256,1,256]{2,0,1:T(8,128)(2,1)} %copy.39), channel_id=1, source_target_pairs={{16,0},{32,16},{48,32},{64,48},{80,64},{96,80},{112,96},{17,1},{33... | collective-permute-start | bytes 393224 | tf_op jit(solution)/shard_map/ppermute | solution.py:19
  32.9 7.7 %collective-permute-start.6 = (f32[8,24,4]{2,1,0:T(8,128)S(1)}, f32[8,24,4]{2,1,0:T(8,128)S(1)}, u32[]{:S(2)}, u32[]{:S(2)}) collective-permute-start(f32[8,24,4]{2,1,0:T(8,128)S(1)} %get-tuple-element.119), channel_id=1, source_target_pairs={{0,1},{1,2},{2,3},{3,4},{4,5},{5,6},{6,7},{7,8},{8,9},{9,10},{10,1... | collective-permute-start | bytes 9224 | tf_op jit(solution)/shard_map/ppermute | solution.py:17
  38.7 7.4 %collective-permute-start.7 = (f32[8,24,4]{2,1,0:T(8,128)S(1)}, f32[8,24,4]{2,1,0:T(8,128)S(1)}, u32[]{:S(2)}, u32[]{:S(2)}) collective-permute-start(f32[8,24,4]{2,1,0:T(8,128)S(1)} %get-tuple-element.120), channel_id=1, source_target_pairs={{1,0},{2,1},{3,2},{4,3},{5,4},{6,5},{7,6},{8,7},{9,8},{10,9},{11,1... | collective-permute-start | bytes 9224 | tf_op jit(solution)/shard_map/ppermute | solution.py:19
  40.6 18.5 %collective-permute-start.20 = (bf16[256,1,256]{2,0,1:T(8,128)(2,1)}, bf16[256,1,256]{2,0,1:T(8,128)(2,1)}, u32[]{:S(2)}, u32[]{:S(2)}) collective-permute-start(bf16[256,1,256]{2,0,1:T(8,128)(2,1)} %copy.38), channel_id=1, source_target_pairs={{0,16},{16,32},{32,48},{48,64},{64,80},{80,96},{96,112},{1,17},{17... | collective-permute-start | bytes 393224 | tf_op jit(solution)/shard_map/ppermute | solution.py:17
  49.6 33.4 %collective-permute-start.3 = (bf16[64,24,4]{2,1,0:T(8,128)(2,1)}, bf16[64,24,4]{2,1,0:T(8,128)(2,1)}, u32[]{:S(2)}, u32[]{:S(2)}) collective-permute-start(bf16[64,24,4]{2,1,0:T(8,128)(2,1)} %get-tuple-element.76), channel_id=1, source_target_pairs={{1,0},{2,1},{3,2},{4,3},{5,4},{6,5},{7,6},{8,7},{9,8},{10,9},{11,1... | collective-permute-start | bytes 36872 | tf_op jit(solution)/shard_map/ppermute | solution.py:19
  51.6 31.5 %collective-permute-start.2 = (bf16[64,24,4]{2,1,0:T(8,128)(2,1)}, bf16[64,24,4]{2,1,0:T(8,128)(2,1)}, u32[]{:S(2)}, u32[]{:S(2)}) collective-permute-start(bf16[64,24,4]{2,1,0:T(8,128)(2,1)} %get-tuple-element.77), channel_id=1, source_target_pairs={{0,1},{1,2},{2,3},{3,4},{4,5},{5,6},{6,7},{7,8},{8,9},{9,10},{10,1... | collective-permute-start | bytes 36872 | tf_op jit(solution)/shard_map/ppermute | solution.py:17
  61.7 11.8 %collective-permute-start.22 = (bf16[256,18,1]{0,1,2:T(8,128)(2,1)S(1)}, bf16[256,18,1]{0,1,2:T(8,128)(2,1)S(1)}, u32[]{:S(2)}, u32[]{:S(2)}) collective-permute-start(bf16[256,18,1]{0,1,2:T(8,128)(2,1)S(1)} %copy.27), channel_id=1, source_target_pairs={{0,1},{1,2},{2,3},{3,4},{4,5},{5,6},{6,7},{7,8},{8,9},{9,10},{10,1... | collective-permute-start | bytes 27656 | tf_op jit(solution)/shard_map/ppermute | solution.py:17
  64.1 9.4 %collective-permute-start.23 = (bf16[256,18,1]{0,1,2:T(8,128)(2,1)S(1)}, bf16[256,18,1]{0,1,2:T(8,128)(2,1)S(1)}, u32[]{:S(2)}, u32[]{:S(2)}) collective-permute-start(bf16[256,18,1]{0,1,2:T(8,128)(2,1)S(1)} %copy.30), channel_id=1, source_target_pairs={{1,0},{2,1},{3,2},{4,3},{5,4},{6,5},{7,6},{8,7},{9,8},{10,9},{11,1... | collective-permute-start | bytes 27656 | tf_op jit(solution)/shard_map/ppermute | solution.py:19
  96.4 5.7 %collective-permute-start.8 = (f32[8,4,256]{2,1,0:T(4,128)S(1)}, f32[8,4,256]{2,1,0:T(4,128)S(1)}, u32[]{:S(2)}, u32[]{:S(2)}) collective-permute-start(f32[8,4,256]{2,1,0:T(4,128)S(1)} %get-tuple-element.125), channel_id=1, source_target_pairs={{0,16},{16,32},{32,48},{48,64},{64,80},{80,96},{96,112},{1,17},{17... | collective-permute-start | bytes 98312 | tf_op jit(solution)/shard_map/ppermute | solution.py:17
  100.0 6.7 %collective-permute-start.9 = (f32[8,4,256]{2,1,0:T(4,128)S(1)}, f32[8,4,256]{2,1,0:T(4,128)S(1)}, u32[]{:S(2)}, u32[]{:S(2)}) collective-permute-start(f32[8,4,256]{2,1,0:T(4,128)S(1)} %get-tuple-element.126), channel_id=1, source_target_pairs={{16,0},{32,16},{48,32},{64,48},{80,64},{96,80},{112,96},{17,1},{33... | collective-permute-start | bytes 98312 | tf_op jit(solution)/shard_map/ppermute | solution.py:19
  106.8 10.4 %collective-permute-start.10 = (f32[8,24,4]{2,1,0:T(8,128)S(1)}, f32[8,24,4]{2,1,0:T(8,128)S(1)}, u32[]{:S(2)}, u32[]{:S(2)}) collective-permute-start(f32[8,24,4]{2,1,0:T(8,128)S(1)} %get-tuple-element.115), channel_id=1, source_target_pairs={{0,1},{1,2},{2,3},{3,4},{4,5},{5,6},{6,7},{7,8},{8,9},{9,10},{10,1... | collective-permute-start | bytes 9224 | tf_op jit(solution)/shard_map/ppermute | solution.py:17
  114.0 7.4 %collective-permute-start.11 = (f32[8,24,4]{2,1,0:T(8,128)S(1)}, f32[8,24,4]{2,1,0:T(8,128)S(1)}, u32[]{:S(2)}, u32[]{:S(2)}) collective-permute-start(f32[8,24,4]{2,1,0:T(8,128)S(1)} %get-tuple-element.116), channel_id=1, source_target_pairs={{1,0},{2,1},{3,2},{4,3},{5,4},{6,5},{7,6},{8,7},{9,8},{10,9},{11,1... | collective-permute-start | bytes 9224 | tf_op jit(solution)/shard_map/ppermute | solution.py:19
  122.3 6.0 %collective-permute-start.12 = (f32[8,4,256]{2,1,0:T(4,128)S(1)}, f32[8,4,256]{2,1,0:T(4,128)S(1)}, u32[]{:S(2)}, u32[]{:S(2)}) collective-permute-start(f32[8,4,256]{2,1,0:T(4,128)S(1)} %get-tuple-element.123), channel_id=1, source_target_pairs={{0,16},{16,32},{32,48},{48,64},{64,80},{80,96},{96,112},{1,17},{17... | collective-permute-start | bytes 98312 | tf_op jit(solution)/shard_map/ppermute | solution.py:17
  131.0 6.6 %collective-permute-start.14 = (f32[8,24,4]{2,1,0:T(8,128)S(1)}, f32[8,24,4]{2,1,0:T(8,128)S(1)}, u32[]{:S(2)}, u32[]{:S(2)}) collective-permute-start(f32[8,24,4]{2,1,0:T(8,128)S(1)} %get-tuple-element.111), channel_id=1, source_target_pairs={{0,1},{1,2},{2,3},{3,4},{4,5},{5,6},{6,7},{7,8},{8,9},{9,10},{10,1... | collective-permute-start | bytes 9224 | tf_op jit(solution)/shard_map/ppermute | solution.py:17
  135.0 8.4 %collective-permute-start.15 = (f32[8,24,4]{2,1,0:T(8,128)S(1)}, f32[8,24,4]{2,1,0:T(8,128)S(1)}, u32[]{:S(2)}, u32[]{:S(2)}) collective-permute-start(f32[8,24,4]{2,1,0:T(8,128)S(1)} %get-tuple-element.112), channel_id=1, source_target_pairs={{1,0},{2,1},{3,2},{4,3},{5,4},{6,5},{7,6},{8,7},{9,8},{10,9},{11,1... | collective-permute-start | bytes 9224 | tf_op jit(solution)/shard_map/ppermute | solution.py:19
  152.0 6.5 %collective-permute-start.18 = (f32[8,24,4]{2,1,0:T(8,128)S(1)}, f32[8,24,4]{2,1,0:T(8,128)S(1)}, u32[]{:S(2)}, u32[]{:S(2)}) collective-permute-start(f32[8,24,4]{2,1,0:T(8,128)S(1)} %get-tuple-element.107), channel_id=1, source_target_pairs={{0,1},{1,2},{2,3},{3,4},{4,5},{5,6},{6,7},{7,8},{8,9},{9,10},{10,1... | collective-permute-start | bytes 9224 | tf_op jit(solution)/shard_map/ppermute | solution.py:17
  155.3 8.1 %collective-permute-start.19 = (f32[8,24,4]{2,1,0:T(8,128)S(1)}, f32[8,24,4]{2,1,0:T(8,128)S(1)}, u32[]{:S(2)}, u32[]{:S(2)}) collective-permute-start(f32[8,24,4]{2,1,0:T(8,128)S(1)} %get-tuple-element.108), channel_id=1, source_target_pairs={{1,0},{2,1},{3,2},{4,3},{5,4},{6,5},{7,6},{8,7},{9,8},{10,9},{11,1... | collective-permute-start | bytes 9224 | tf_op jit(solution)/shard_map/ppermute | solution.py:19
  254.0 8.7 %collective-permute-start.25 = (bf16[256,1,256]{0,2,1:T(8,128)(2,1)S(1)}, bf16[256,1,256]{0,2,1:T(8,128)(2,1)S(1)}, u32[]{:S(2)}, u32[]{:S(2)}) collective-permute-start(bf16[256,1,256]{0,2,1:T(8,128)(2,1)S(1)} %get-tuple-element.69), channel_id=1, source_target_pairs={{16,0},{32,16},{48,32},{64,48},{80,64},{96,80},{112,96},{17,1},{33... | collective-permute-start | bytes 393224 | tf_op jit(solution)/shard_map/ppermute | solution.py:19
  262.8 8.5 %collective-permute-start.26 = (bf16[256,18,1]{0,2,1:T(2,128)(2,1)S(1)}, bf16[256,18,1]{0,2,1:T(2,128)(2,1)S(1)}, u32[]{:S(2)}, u32[]{:S(2)}) collective-permute-start(bf16[256,18,1]{0,2,1:T(2,128)(2,1)S(1)} %get-tuple-element.60), channel_id=1, source_target_pairs={{1,0},{2,1},{3,2},{4,3},{5,4},{6,5},{7,6},{8,7},{9,8},{10,9},{11,1... | collective-permute-start | bytes 27656 | tf_op jit(solution)/shard_map/ppermute | solution.py:19
  (38 other events, 721.5 us)
Sparse Core Ops, SparseCore 0:
  252.5 148.9 all-reduce.1
where the time goes:
time: 420 us; the launch traced here: 412 us
  waiting for transfers between devices  150 us (36%)
  starting transfers between devices  81.9 us (20%)
  blocking collectives  69.5 us (17%)
  local copies, waits for them, and re-layouts  34.8 us (8%)
  matrix products  31.9 us (8%)
  other arithmetic  28.1 us (7%)
  between operations  15.4 us (4%)
    psum x1, waiting for transfers between devices, shards(): lax.psum((jnp.stack(conv_parts), class_part), ('row', 'col'))  118 us
    psum x1, blocking collectives, shards(): lax.psum((jnp.stack(conv_parts), class_part), ('row', 'col'))  69.5 us
    ppermute x14, starting transfers between devices, with_halo(): lax.ppermute(tail, axis, [(i, (i + 1) % count) for i in range(ends)])  57.9 us
    ppermute x14, waiting for transfers between devices, with_halo(): lax.ppermute(head, axis, [((i + 1) % count, i) for i in range(ends)])  32.3 us
    ppermute x14, starting transfers between devices, with_halo(): lax.ppermute(head, axis, [((i + 1) % count, i) for i in range(ends)])  23.9 us
    unnamed x77, local copies, waits for them, and re-layouts  16.6 us
    dot_general x9, matrix products, shards(): jnp.einsum('cp,hp->ch', shifted, back_error, preferred_element_type=jnp.f...  14.6 us
    concatenate x15, other arithmetic, with_halo(): jnp.concatenate([lax.ppermute(tail, axis, [(i, (i + 1) % count) for i in...  12.9 us
  transfers between devices with their start and end apart: 29, of which 10 were waited for; matrix products, arithmetic and copies ran while one was open for 13% of the time, Pallas kernels for 0%

commit v1 on v0

--- a/solution.py
+++ b/solution.py
@@ -84,6 +84,67 @@
             padded, 4, off_y, off_x, span_y, span_x
         )
     return running
+
+
+def split_chunks(conv_part, class_part, devices):
+    taps, channels, hidden = conv_part.shape
+    tiles = conv_part.reshape(taps, channels // 8, 8, hidden // 128, 128).transpose(0, 1, 3, 2, 4)
+    tiles = tiles.reshape(-1, 8, 128)
+    whole = (tiles.shape[0] // devices) * devices
+    head = tiles[:whole].reshape(devices, -1, 128)
+    rest = tiles[whole:].reshape(devices, -1, 128)
+    small = class_part.reshape(devices, -1)
+    small = jnp.pad(small, ((0, 0), (0, 128 - small.shape[1])))[:, None, :]
+    return head, rest, small
+
+
+def join_chunks(chunks, shapes, devices):
+    conv_shape, class_shape = shapes
+    taps, channels, hidden = conv_shape
+    n_tiles = taps * channels * hidden // 1024
+    head_rows = (n_tiles // devices) * 8
+    conv_rows = n_tiles * 8 // devices
+    head = chunks[:, :head_rows].reshape(-1, 8, 128)
+    rest = chunks[:, head_rows:conv_rows].reshape(-1, 8, 128)
+    tiles = jnp.concatenate([head, rest], axis=0)
+    tiles = tiles.reshape(taps, channels // 8, hidden // 128, 8, 128).transpose(0, 1, 3, 2, 4)
+    small = chunks[:, conv_rows, : class_shape[0] * class_shape[1] // devices]
+    return tiles.reshape(conv_shape), small.reshape(class_shape)
+
+
+def shift_of(largest):
+    return jnp.clip(jnp.ceil(jnp.log2(jnp.maximum(largest, 1e-30))), -100.0, 120.0)
+
+
+def pack_half(values, exponent):
+    scaled = (values * jnp.exp2(14.0 - exponent)).astype(jnp.float16)
+    marks = jnp.broadcast_to(exponent, values.shape[:-2] + (1, 128)).astype(jnp.float16)
+    rows = values.shape[-2]
+    fill = -(-(rows + 1) // 8) * 8 - rows - 1
+    zeros = jnp.zeros(values.shape[:-2] + (fill, 128), jnp.float16)
+    return jnp.concatenate([scaled, marks, zeros], axis=-2)
+
+
+def unpack_half(packed, rows):
+    exponent = packed[..., rows : rows + 1, :1].astype(jnp.float32)
+    return packed[..., :rows, :].astype(jnp.float32) * jnp.exp2(exponent - 14.0)
+
+
+def sum_everywhere(conv_part, class_part, axes):
+    devices = 1
+    for axis in axes:
+        devices = devices * lax.axis_size(axis)
+    head, rest, small = split_chunks(conv_part, class_part, devices)
+    values = jnp.concatenate([head, rest, small], axis=1)
+    rows = values.shape[1]
+    largest = jnp.maximum(jnp.max(jnp.abs(conv_part)), jnp.max(jnp.abs(class_part)))
+    sent = pack_half(values, shift_of(largest))
+    got = lax.all_to_all(sent, axes, split_axis=0, concat_axis=0, tiled=True)
+    total = jnp.sum(unpack_half(got, rows), axis=0)
+    mine = pack_half(total, shift_of(jnp.max(jnp.abs(total))))
+    spread = jnp.broadcast_to(mine[None], (devices,) + mine.shape)
+    everyone = lax.all_to_all(spread, axes, split_axis=0, concat_axis=0, tiled=True)
+    return join_chunks(unpack_half(everyone, rows), (conv_part.shape, class_part.shape), devices)
 
 
 def shards(teacher_feats, teacher_probs, student_feats, conv_weight, class_weight):
@@ -134,7 +195,9 @@
             "ch,hp->cp", conv_weight[tap_index], moved, preferred_element_type=jnp.float32
         )
     feature_grad = feature_sum.astype(jnp.bfloat16).reshape(channels, rows_here, cols_here)
-    summed_conv, summed_class = lax.psum((jnp.stack(conv_parts), class_part), ("row", "col"))
+    summed_conv, summed_class = sum_everywhere(
+        jnp.stack(conv_parts), class_part, ("row", "col")
+    )
     grad_conv = summed_conv / pixel_count
     grad_class = summed_class / pixel_count
     return (current, feature_grad, grad_conv, grad_class)

time: 420 us -> 276 us (0.66); the launches traced: 412 us -> 273 us
  waiting for transfers between devices: 150 us -> 46.9 us
  blocking collectives: 69.5 us -> 0 us
  starting transfers between devices: 81.9 us -> 104 us
  other arithmetic: 28.1 us -> 46.2 us
  between operations: 15.4 us -> 4.3 us
  local copies, waits for them, and re-layouts: 34.8 us -> 42 us
    psum x1 -> x0, waiting for transfers between devices: 118 us -> none  [shards(): lax.psum((jnp.stack(conv_parts), class_part), ('row', 'col'))]
    psum x1 -> x0, blocking collectives: 69.5 us -> none  [shards(): lax.psum((jnp.stack(conv_parts), class_part), ('row', 'col'))]
    all_to_all x0 -> x2, starting transfers between devices: none -> 21.1 us  [the longest x1 13 us: sum_everywhere(): got = lax.all_to_all(sent, axes, split_axis=0, concat_axis=0, tiled=True)]
    concatenate x15, other arithmetic: 12.9 us -> 26.6 us  [with_halo(): jnp.concatenate([lax.ppermute(tail, axis, [(i, (i + 1) % count) for i in...]
    all_to_all x0 -> x2, waiting for transfers between devices: none -> 12.4 us  [the longest x1 12.4 us: sum_everywhere(): lax.all_to_all(spread, axes, split_axis=0, concat_axis=0, tiled=True)]
    dot_general x9, matrix products: 14.6 us -> 6.8 us  [shards(): jnp.einsum('cp,hp->ch', shifted, back_error, preferred_element_type=jnp.f...]
    dot_general x9, matrix products: 7.02 us -> 11.8 us  [shards(): jnp.einsum('ch,hp->cp', conv_weight[tap_index], moved, preferred_element_...]
    unnamed x77 -> x68, local copies, waits for them, and re-layouts: 16.6 us -> 16.5 us
  transfers between devices with their start and end apart: 29 -> 30, of which waited for: 10 -> 9; matrix products, arithmetic and copies ran while one was open for 13% -> 29% of each run, Pallas kernels for 0% -> 0%
where the time goes in v1:
time: 276 us; the launch traced here: 273 us
  starting transfers between devices  104 us (38%)
  waiting for transfers between devices  46.9 us (17%)
  other arithmetic  46.2 us (17%)
  local copies, waits for them, and re-layouts  42 us (15%)
  matrix products  29.4 us (11%)
  between operations  4.3 us (2%)
    ppermute x14, starting transfers between devices, with_halo(): lax.ppermute(tail, axis, [(i, (i + 1) % count) for i in range(ends)])  58.1 us
    ppermute x14, waiting for transfers between devices, with_halo(): lax.ppermute(head, axis, [((i + 1) % count, i) for i in range(ends)])  34.4 us
    concatenate x15, other arithmetic, with_halo(): jnp.concatenate([lax.ppermute(tail, axis, [(i, (i + 1) % count) for i in...  26.6 us
    ppermute x14, starting transfers between devices, with_halo(): lax.ppermute(head, axis, [((i + 1) % count, i) for i in range(ends)])  25.2 us
    unnamed x68, local copies, waits for them, and re-layouts  16.5 us
    all_to_all x1, starting transfers between devices, sum_everywhere(): got = lax.all_to_all(sent, axes, split_axis=0, concat_axis=0, tiled=True)  13 us
    all_to_all x1, waiting for transfers between devices, sum_everywhere(): lax.all_to_all(spread, axes, split_axis=0, concat_axis=0, tiled=True)  12.4 us
    dot_general x9, matrix products, shards(): jnp.einsum('ch,hp->cp', conv_weight[tap_index], moved, preferred_element_...  11.8 us
  transfers between devices with their start and end apart: 30, of which 9 were waited for; matrix products, arithmetic and copies ran while one was open for 29% of the time, Pallas kernels for 0%

profile of v1, /device:TPU:1, one launch (start us, length us, event | category | flops | bytes accessed | tf_op | source)
XLA Modules:
  0.0 273.3 jit_solution(13454686278364510106)
XLA Ops:
  2.7 3.9 %collective-permute-start = (bf16[64,4,256]{2,1,0:T(4,128)(2,1)}, bf16[64,4,256]{2,1,0:T(4,128)(2,1)S(1)}, u32[]{:S(2)}, u32[]{:S(2)}) collective-permute-start(bf16[64,4,256]{2,1,0:T(4,128)(2,1)} %get-tuple-element.94), channel_id=1, source_target_pairs={{0,16},{16,32},{32,48},{48,64},{64,80},{80,96},{96,112},{1,17},{17... | collective-permute-start | bytes 393224 | tf_op jit(solution)/shard_map/ppermute | solution.py:17
  8.8 4.0 %collective-permute-start.4 = (f32[8,4,256]{2,1,0:T(4,128)S(1)}, f32[8,4,256]{2,1,0:T(4,128)S(1)}, u32[]{:S(2)}, u32[]{:S(2)}) collective-permute-start(f32[8,4,256]{2,1,0:T(4,128)S(1)} %get-tuple-element.144), channel_id=1, source_target_pairs={{0,16},{16,32},{32,48},{48,64},{64,80},{80,96},{96,112},{1,17},{17... | collective-permute-start | bytes 98312 | tf_op jit(solution)/shard_map/ppermute | solution.py:17
  16.7 5.3 %collective-permute-start.20 = (bf16[256,1,256]{2,0,1:T(8,128)(2,1)}, bf16[256,1,256]{2,0,1:T(8,128)(2,1)}, u32[]{:S(2)}, u32[]{:S(2)}) collective-permute-start(bf16[256,1,256]{2,0,1:T(8,128)(2,1)} %copy.92), channel_id=1, source_target_pairs={{0,16},{16,32},{32,48},{48,64},{64,80},{80,96},{96,112},{1,17},{17... | collective-permute-start | bytes 393224 | tf_op jit(solution)/shard_map/ppermute | solution.py:17
  29.5 6.3 %collective-permute-start.6 = (f32[8,24,4]{2,1,0:T(8,128)S(1)}, f32[8,24,4]{2,1,0:T(8,128)S(1)}, u32[]{:S(2)}, u32[]{:S(2)}) collective-permute-start(f32[8,24,4]{2,1,0:T(8,128)S(1)} %get-tuple-element.135), channel_id=1, source_target_pairs={{0,1},{1,2},{2,3},{3,4},{4,5},{5,6},{6,7},{7,8},{8,9},{9,10},{10,1... | collective-permute-start | bytes 9224 | tf_op jit(solution)/shard_map/ppermute | solution.py:17
  39.1 4.2 %collective-permute-done.7 = f32[8,24,4]{2,1,0:T(8,128)S(1)} collective-permute-done((f32[8,24,4]{2,1,0:T(8,128)S(1)}, f32[8,24,4]{2,1,0:T(8,128)S(1)}, u32[]{:S(2)}, u32[]{:S(2)}) %collective-permute-start.7) | collective-permute-done | bytes 3104 | tf_op jit(solution)/shard_map/ppermute | solution.py:19
  56.2 3.9 %collective-permute-start.22 = (bf16[256,18,1]{0,1,2:T(8,128)(2,1)S(1)}, bf16[256,18,1]{0,1,2:T(8,128)(2,1)S(1)}, u32[]{:S(2)}, u32[]{:S(2)}) collective-permute-start(bf16[256,18,1]{0,1,2:T(8,128)(2,1)S(1)} %copy.77), channel_id=1, source_target_pairs={{0,1},{1,2},{2,3},{3,4},{4,5},{5,6},{6,7},{7,8},{8,9},{9,10},{10,1... | collective-permute-start | bytes 27656 | tf_op jit(solution)/shard_map/ppermute | solution.py:17
  70.0 12.8 %pad_maximum_fusion = (bf16[256,18,257]{0,2,1:T(8,128)(2,1)S(1)}, bf16[256,18,257]{0,2,1:T(8,128)(2,1)S(1)}) fusion(bf16[256,18,1]{0,2,1:T(2,128)(2,1)S(1)} %copy.81, bf16[256,1,256]{0,2,1:T(8,128)(2,1)S(1)} %copy-done.19, bf16[256,16,256]{0,2,1:T(8,128)(2,1)S(1)} %copy-done.3, bf16[256,1,256]{0,2,1:T(8,128)(2,1)S(1)} %copy-done.18, ...), kind=kLoop, calls=%fused_computation.63 | loop fusion | flops 18948096 | bytes 7114752 | tf_op jit(solution)/shard_map/concatenate | solution.py:15
  82.9 3.4 %fusion.243 = (bf16[256,16,256]{0,2,1:T(8,128)(2,1)S(1)}, bf16[256,16,256]{0,2,1:T(8,128)(2,1)S(1)}, bf16[256,16,256]{0,2,1:T(8,128)(2,1)S(1)}, bf16[256,16,256]...) fusion(bf16[256,18,257]{0,2,1:T(8,128)(2,1)S(1)} %get-tuple-element.78, ...), kind=kLoop, calls=%fused_computation.544 | loop fusion | bytes 25165824 | tf_op jit(solution)/shard_map/slice | solution.py:41
  94.2 4.3 %fusion.63 = (f32[16,256]{1,0:T(8,128)S(1)}, f32[16,256]{1,0:T(8,128)S(1)}, f32[16,256]{1,0:T(8,128)S(1)}, f32[16,256]{1,0:T(8,128)S(1)}, f32[16,256]{1,0:T(8,12...) fusion(bf16[64,16,256]{2,1,0:T(8,128)(2,1)S(1)} %copy-done.6, ...), kind=kLoop, calls=%fused_computation.122 | loop fusion | flops 18288640 | bytes 7192576 | tf_op jit(solution)/shard_map/reduce_sum | solution.py:71
  101.0 4.6 %collective-permute-start.8 = (f32[8,4,256]{2,1,0:T(4,128)S(1)}, f32[8,4,256]{2,1,0:T(4,128)S(1)}, u32[]{:S(2)}, u32[]{:S(2)}) collective-permute-start(f32[8,4,256]{2,1,0:T(4,128)S(1)} %get-tuple-element.141), channel_id=1, source_target_pairs={{0,16},{16,32},{32,48},{48,64},{64,80},{80,96},{96,112},{1,17},{17... | collective-permute-start | bytes 98312 | tf_op jit(solution)/shard_map/ppermute | solution.py:17
  107.6 3.2 %collective-permute-done.9 = f32[8,4,256]{2,1,0:T(4,128)S(1)} collective-permute-done((f32[8,4,256]{2,1,0:T(4,128)S(1)}, f32[8,4,256]{2,1,0:T(4,128)S(1)}, u32[]{:S(2)}, u32[]{:S(2)}) %collective-permute-start.9) | collective-permute-done | bytes 32800 | tf_op jit(solution)/shard_map/ppermute | solution.py:19
  110.9 6.6 %collective-permute-start.10 = (f32[8,24,4]{2,1,0:T(8,128)S(1)}, f32[8,24,4]{2,1,0:T(8,128)S(1)}, u32[]{:S(2)}, u32[]{:S(2)}) collective-permute-start(f32[8,24,4]{2,1,0:T(8,128)S(1)} %get-tuple-element.131), channel_id=1, source_target_pairs={{0,1},{1,2},{2,3},{3,4},{4,5},{5,6},{6,7},{7,8},{8,9},{9,10},{10,1... | collective-permute-start | bytes 9224 | tf_op jit(solution)/shard_map/ppermute | solution.py:17
  120.5 4.5 %collective-permute-done.11 = f32[8,24,4]{2,1,0:T(8,128)S(1)} collective-permute-done((f32[8,24,4]{2,1,0:T(8,128)S(1)}, f32[8,24,4]{2,1,0:T(8,128)S(1)}, u32[]{:S(2)}, u32[]{:S(2)}) %collective-permute-start.11) | collective-permute-done | bytes 3104 | tf_op jit(solution)/shard_map/ppermute | solution.py:19
  125.9 4.0 %collective-permute-start.12 = (f32[8,4,256]{2,1,0:T(4,128)S(1)}, f32[8,4,256]{2,1,0:T(4,128)S(1)}, u32[]{:S(2)}, u32[]{:S(2)}) collective-permute-start(f32[8,4,256]{2,1,0:T(4,128)S(1)} %get-tuple-element.139), channel_id=1, source_target_pairs={{0,16},{16,32},{32,48},{48,64},{64,80},{80,96},{96,112},{1,17},{17... | collective-permute-start | bytes 98312 | tf_op jit(solution)/shard_map/ppermute | solution.py:17
  134.7 4.0 %collective-permute-start.14 = (f32[8,24,4]{2,1,0:T(8,128)S(1)}, f32[8,24,4]{2,1,0:T(8,128)S(1)}, u32[]{:S(2)}, u32[]{:S(2)}) collective-permute-start(f32[8,24,4]{2,1,0:T(8,128)S(1)} %get-tuple-element.127), channel_id=1, source_target_pairs={{0,1},{1,2},{2,3},{3,4},{4,5},{5,6},{6,7},{7,8},{8,9},{9,10},{10,1... | collective-permute-start | bytes 9224 | tf_op jit(solution)/shard_map/ppermute | solution.py:17
  141.4 5.7 %collective-permute-done.15 = f32[8,24,4]{2,1,0:T(8,128)S(1)} collective-permute-done((f32[8,24,4]{2,1,0:T(8,128)S(1)}, f32[8,24,4]{2,1,0:T(8,128)S(1)}, u32[]{:S(2)}, u32[]{:S(2)}) %collective-permute-start.15) | collective-permute-done | bytes 3104 | tf_op jit(solution)/shard_map/ppermute | solution.py:19
  155.7 3.3 %collective-permute-start.18 = (f32[8,24,4]{2,1,0:T(8,128)S(1)}, f32[8,24,4]{2,1,0:T(8,128)S(1)}, u32[]{:S(2)}, u32[]{:S(2)}) collective-permute-start(f32[8,24,4]{2,1,0:T(8,128)S(1)} %get-tuple-element.123), channel_id=1, source_target_pairs={{0,1},{1,2},{2,3},{3,4},{4,5},{5,6},{6,7},{7,8},{8,9},{9,10},{10,1... | collective-permute-start | bytes 9224 | tf_op jit(solution)/shard_map/ppermute | solution.py:17
  162.6 4.5 %collective-permute-done.19 = f32[8,24,4]{2,1,0:T(8,128)S(1)} collective-permute-done((f32[8,24,4]{2,1,0:T(8,128)S(1)}, f32[8,24,4]{2,1,0:T(8,128)S(1)}, u32[]{:S(2)}, u32[]{:S(2)}) %collective-permute-start.19) | collective-permute-done | bytes 3104 | tf_op jit(solution)/shard_map/ppermute | solution.py:19
  184.1 3.6 %collective-permute-start.24 = (bf16[256,1,256]{0,2,1:T(8,128)(2,1)}, bf16[256,1,256]{0,2,1:T(8,128)(2,1)S(1)}, u32[]{:S(2)}, u32[]{:S(2)}) collective-permute-start(bf16[256,1,256]{0,2,1:T(8,128)(2,1)} %get-tuple-element.84), channel_id=1, source_target_pairs={{0,16},{16,32},{32,48},{48,64},{64,80},{80,96},{96,112},{1,17},{17... | collective-permute-start | bytes 393224 | tf_op jit(solution)/shard_map/ppermute | solution.py:17
  192.6 13.0 %all-to-all-start = ((f16[128,40,128]{2,1,0:T(8,128)(2,1)}), f16[128,40,128]{2,1,0:T(8,128)(2,1)S(1)}, u32[]{:S(2)}, u32[]{:S(2)}) async-start(f16[128,40,128]{2,1,0:T(8,128)(2,1)} %maximum_maximum_fusion.2), calls=%async_computation | async-start | bytes 2621440 | tf_op jit(solution)/shard_map/all_to_all | solution.py:142
  209.4 4.2 %collective-permute-start.27 = (bf16[256,18,1]{0,2,1:T(2,128)(2,1)S(1)}, bf16[256,18,1]{0,2,1:T(2,128)(2,1)S(1)}, u32[]{:S(2)}, u32[]{:S(2)}) collective-permute-start(bf16[256,18,1]{0,2,1:T(2,128)(2,1)S(1)} %get-tuple-element.77), channel_id=1, source_target_pairs={{0,1},{1,2},{2,3},{3,4},{4,5},{5,6},{6,7},{7,8},{8,9},{9,10},{10,1... | collective-permute-start | bytes 27656 | tf_op jit(solution)/shard_map/ppermute | solution.py:17
  217.0 6.6 %collective-permute-done.26 = bf16[256,18,1]{0,2,1:T(2,128)(2,1)S(1)} collective-permute-done((bf16[256,18,1]{0,2,1:T(2,128)(2,1)S(1)}, bf16[256,18,1]{0,2,1:T(2,128)(2,1)S(1)}, u32[]{:S(2)}, u32[]{:S(2)}) %collective-permute-start.26) | collective-permute-done | bytes 9248 | tf_op jit(solution)/shard_map/ppermute | solution.py:19
  239.6 8.1 %all-to-all-start.1 = ((f16[128,40,128]{2,1,0:T(8,128)(2,1)}), f16[128,40,128]{2,1,0:T(8,128)(2,1)S(1)}, u32[]{:S(2)}, u32[]{:S(2)}) async-start(f16[128,40,128]{2,1,0:T(8,128)(2,1)} %broadcast_in_dim.29), calls=%async_computation.1 | async-start | bytes 2621440 | tf_op jit(solution)/shard_map/all_to_all | solution.py:146
  257.2 12.4 %all-to-all-done.1 = f16[128,40,128]{2,1,0:T(8,128)(2,1)S(1)} async-done(((f16[128,40,128]{2,1,0:T(8,128)(2,1)}), f16[128,40,128]{2,1,0:T(8,128)(2,1)S(1)}, u32[]{:S(2)}, u32[]{:S(2)}) %all-to-all-start.1) | async-done | bytes 1310752 | tf_op jit(solution)/shard_map/all_to_all | solution.py:146
  (240 shorter events, 132.5 us)
Async XLA Ops:
  2.7 41.7 %collective-permute-start = (bf16[64,4,256]{2,1,0:T(4,128)(2,1)}, bf16[64,4,256]{2,1,0:T(4,128)(2,1)S(1)}, u32[]{:S(2)}, u32[]{:S(2)}) collective-permute-start(bf16[64,4,256]{2,1,0:T(4,128)(2,1)} %get-tuple-element.94), channel_id=1, source_target_pairs={{0,16},{16,32},{32,48},{48,64},{64,80},{80,96},{96,112},{1,17},{17... | collective-permute-start | bytes 393224 | tf_op jit(solution)/shard_map/ppermute | solution.py:17
  6.6 37.7 %collective-permute-start.1 = (bf16[64,4,256]{2,1,0:T(4,128)(2,1)}, bf16[64,4,256]{2,1,0:T(4,128)(2,1)}, u32[]{:S(2)}, u32[]{:S(2)}) collective-permute-start(bf16[64,4,256]{2,1,0:T(4,128)(2,1)} %get-tuple-element.95), channel_id=1, source_target_pairs={{16,0},{32,16},{48,32},{64,48},{80,64},{96,80},{112,96},{17,1},{33... | collective-permute-start | bytes 393224 | tf_op jit(solution)/shard_map/ppermute | solution.py:19
  8.8 20.6 %collective-permute-start.4 = (f32[8,4,256]{2,1,0:T(4,128)S(1)}, f32[8,4,256]{2,1,0:T(4,128)S(1)}, u32[]{:S(2)}, u32[]{:S(2)}) collective-permute-start(f32[8,4,256]{2,1,0:T(4,128)S(1)} %get-tuple-element.144), channel_id=1, source_target_pairs={{0,16},{16,32},{32,48},{48,64},{64,80},{80,96},{96,112},{1,17},{17... | collective-permute-start | bytes 98312 | tf_op jit(solution)/shard_map/ppermute | solution.py:17
  12.8 16.6 %collective-permute-start.5 = (f32[8,4,256]{2,1,0:T(4,128)S(1)}, f32[8,4,256]{2,1,0:T(4,128)S(1)}, u32[]{:S(2)}, u32[]{:S(2)}) collective-permute-start(f32[8,4,256]{2,1,0:T(4,128)S(1)} %get-tuple-element.143), channel_id=1, source_target_pairs={{16,0},{32,16},{48,32},{64,48},{80,64},{96,80},{112,96},{17,1},{33... | collective-permute-start | bytes 98312 | tf_op jit(solution)/shard_map/ppermute | solution.py:19
  16.7 35.2 %collective-permute-start.20 = (bf16[256,1,256]{2,0,1:T(8,128)(2,1)}, bf16[256,1,256]{2,0,1:T(8,128)(2,1)}, u32[]{:S(2)}, u32[]{:S(2)}) collective-permute-start(bf16[256,1,256]{2,0,1:T(8,128)(2,1)} %copy.92), channel_id=1, source_target_pairs={{0,16},{16,32},{32,48},{48,64},{64,80},{80,96},{96,112},{1,17},{17... | collective-permute-start | bytes 393224 | tf_op jit(solution)/shard_map/ppermute | solution.py:17
  29.5 8.3 %collective-permute-start.6 = (f32[8,24,4]{2,1,0:T(8,128)S(1)}, f32[8,24,4]{2,1,0:T(8,128)S(1)}, u32[]{:S(2)}, u32[]{:S(2)}) collective-permute-start(f32[8,24,4]{2,1,0:T(8,128)S(1)} %get-tuple-element.135), channel_id=1, source_target_pairs={{0,1},{1,2},{2,3},{3,4},{4,5},{5,6},{6,7},{7,8},{8,9},{9,10},{10,1... | collective-permute-start | bytes 9224 | tf_op jit(solution)/shard_map/ppermute | solution.py:17
  35.9 7.4 %collective-permute-start.7 = (f32[8,24,4]{2,1,0:T(8,128)S(1)}, f32[8,24,4]{2,1,0:T(8,128)S(1)}, u32[]{:S(2)}, u32[]{:S(2)}) collective-permute-start(f32[8,24,4]{2,1,0:T(8,128)S(1)} %get-tuple-element.136), channel_id=1, source_target_pairs={{1,0},{2,1},{3,2},{4,3},{5,4},{6,5},{7,6},{8,7},{9,8},{10,9},{11,1... | collective-permute-start | bytes 9224 | tf_op jit(solution)/shard_map/ppermute | solution.py:19
  37.8 15.8 %collective-permute-start.21 = (bf16[256,1,256]{2,0,1:T(8,128)(2,1)}, bf16[256,1,256]{2,0,1:T(8,128)(2,1)}, u32[]{:S(2)}, u32[]{:S(2)}) collective-permute-start(bf16[256,1,256]{2,0,1:T(8,128)(2,1)} %copy.93), channel_id=1, source_target_pairs={{16,0},{32,16},{48,32},{64,48},{80,64},{96,80},{112,96},{17,1},{33... | collective-permute-start | bytes 393224 | tf_op jit(solution)/shard_map/ppermute | solution.py:19
  46.8 41.6 %collective-permute-start.2 = (bf16[64,24,4]{2,1,0:T(8,128)(2,1)}, bf16[64,24,4]{2,1,0:T(8,128)(2,1)}, u32[]{:S(2)}, u32[]{:S(2)}) collective-permute-start(bf16[64,24,4]{2,1,0:T(8,128)(2,1)} %get-tuple-element.93), channel_id=1, source_target_pairs={{0,1},{1,2},{2,3},{3,4},{4,5},{5,6},{6,7},{7,8},{8,9},{9,10},{10,1... | collective-permute-start | bytes 36872 | tf_op jit(solution)/shard_map/ppermute | solution.py:17
  48.8 39.7 %collective-permute-start.3 = (bf16[64,24,4]{2,1,0:T(8,128)(2,1)}, bf16[64,24,4]{2,1,0:T(8,128)(2,1)}, u32[]{:S(2)}, u32[]{:S(2)}) collective-permute-start(bf16[64,24,4]{2,1,0:T(8,128)(2,1)} %get-tuple-element.92), channel_id=1, source_target_pairs={{1,0},{2,1},{3,2},{4,3},{5,4},{6,5},{7,6},{8,7},{9,8},{10,9},{11,1... | collective-permute-start | bytes 36872 | tf_op jit(solution)/shard_map/ppermute | solution.py:19
  56.2 13.2 %collective-permute-start.22 = (bf16[256,18,1]{0,1,2:T(8,128)(2,1)S(1)}, bf16[256,18,1]{0,1,2:T(8,128)(2,1)S(1)}, u32[]{:S(2)}, u32[]{:S(2)}) collective-permute-start(bf16[256,18,1]{0,1,2:T(8,128)(2,1)S(1)} %copy.77), channel_id=1, source_target_pairs={{0,1},{1,2},{2,3},{3,4},{4,5},{5,6},{6,7},{7,8},{8,9},{9,10},{10,1... | collective-permute-start | bytes 27656 | tf_op jit(solution)/shard_map/ppermute | solution.py:17
  60.2 9.3 %collective-permute-start.23 = (bf16[256,18,1]{0,1,2:T(8,128)(2,1)S(1)}, bf16[256,18,1]{0,1,2:T(8,128)(2,1)S(1)}, u32[]{:S(2)}, u32[]{:S(2)}) collective-permute-start(bf16[256,18,1]{0,1,2:T(8,128)(2,1)S(1)} %copy.80), channel_id=1, source_target_pairs={{1,0},{2,1},{3,2},{4,3},{5,4},{6,5},{7,6},{8,7},{9,8},{10,9},{11,1... | collective-permute-start | bytes 27656 | tf_op jit(solution)/shard_map/ppermute | solution.py:19
  110.9 9.6 %collective-permute-start.10 = (f32[8,24,4]{2,1,0:T(8,128)S(1)}, f32[8,24,4]{2,1,0:T(8,128)S(1)}, u32[]{:S(2)}, u32[]{:S(2)}) collective-permute-start(f32[8,24,4]{2,1,0:T(8,128)S(1)} %get-tuple-element.131), channel_id=1, source_target_pairs={{0,1},{1,2},{2,3},{3,4},{4,5},{5,6},{6,7},{7,8},{8,9},{9,10},{10,1... | collective-permute-start | bytes 9224 | tf_op jit(solution)/shard_map/ppermute | solution.py:17
  117.6 7.4 %collective-permute-start.11 = (f32[8,24,4]{2,1,0:T(8,128)S(1)}, f32[8,24,4]{2,1,0:T(8,128)S(1)}, u32[]{:S(2)}, u32[]{:S(2)}) collective-permute-start(f32[8,24,4]{2,1,0:T(8,128)S(1)} %get-tuple-element.132), channel_id=1, source_target_pairs={{1,0},{2,1},{3,2},{4,3},{5,4},{6,5},{7,6},{8,7},{9,8},{10,9},{11,1... | collective-permute-start | bytes 9224 | tf_op jit(solution)/shard_map/ppermute | solution.py:19
  134.7 6.7 %collective-permute-start.14 = (f32[8,24,4]{2,1,0:T(8,128)S(1)}, f32[8,24,4]{2,1,0:T(8,128)S(1)}, u32[]{:S(2)}, u32[]{:S(2)}) collective-permute-start(f32[8,24,4]{2,1,0:T(8,128)S(1)} %get-tuple-element.127), channel_id=1, source_target_pairs={{0,1},{1,2},{2,3},{3,4},{4,5},{5,6},{6,7},{7,8},{8,9},{9,10},{10,1... | collective-permute-start | bytes 9224 | tf_op jit(solution)/shard_map/ppermute | solution.py:17
  138.7 8.4 %collective-permute-start.15 = (f32[8,24,4]{2,1,0:T(8,128)S(1)}, f32[8,24,4]{2,1,0:T(8,128)S(1)}, u32[]{:S(2)}, u32[]{:S(2)}) collective-permute-start(f32[8,24,4]{2,1,0:T(8,128)S(1)} %get-tuple-element.128), channel_id=1, source_target_pairs={{1,0},{2,1},{3,2},{4,3},{5,4},{6,5},{7,6},{8,7},{9,8},{10,9},{11,1... | collective-permute-start | bytes 9224 | tf_op jit(solution)/shard_map/ppermute | solution.py:19
  155.7 6.9 %collective-permute-start.18 = (f32[8,24,4]{2,1,0:T(8,128)S(1)}, f32[8,24,4]{2,1,0:T(8,128)S(1)}, u32[]{:S(2)}, u32[]{:S(2)}) collective-permute-start(f32[8,24,4]{2,1,0:T(8,128)S(1)} %get-tuple-element.123), channel_id=1, source_target_pairs={{0,1},{1,2},{2,3},{3,4},{4,5},{5,6},{6,7},{7,8},{8,9},{9,10},{10,1... | collective-permute-start | bytes 9224 | tf_op jit(solution)/shard_map/ppermute | solution.py:17
  159.0 8.2 %collective-permute-start.19 = (f32[8,24,4]{2,1,0:T(8,128)S(1)}, f32[8,24,4]{2,1,0:T(8,128)S(1)}, u32[]{:S(2)}, u32[]{:S(2)}) collective-permute-start(f32[8,24,4]{2,1,0:T(8,128)S(1)} %get-tuple-element.124), channel_id=1, source_target_pairs={{1,0},{2,1},{3,2},{4,3},{5,4},{6,5},{7,6},{8,7},{9,8},{10,9},{11,1... | collective-permute-start | bytes 9224 | tf_op jit(solution)/shard_map/ppermute | solution.py:19
  184.1 21.5 %collective-permute-start.24 = (bf16[256,1,256]{0,2,1:T(8,128)(2,1)}, bf16[256,1,256]{0,2,1:T(8,128)(2,1)S(1)}, u32[]{:S(2)}, u32[]{:S(2)}) collective-permute-start(bf16[256,1,256]{0,2,1:T(8,128)(2,1)} %get-tuple-element.84), channel_id=1, source_target_pairs={{0,16},{16,32},{32,48},{48,64},{64,80},{80,96},{96,112},{1,17},{17... | collective-permute-start | bytes 393224 | tf_op jit(solution)/shard_map/ppermute | solution.py:17
  187.7 17.9 %collective-permute-start.25 = (bf16[256,1,256]{0,2,1:T(8,128)(2,1)}, bf16[256,1,256]{0,2,1:T(8,128)(2,1)}, u32[]{:S(2)}, u32[]{:S(2)}) collective-permute-start(bf16[256,1,256]{0,2,1:T(8,128)(2,1)} %get-tuple-element.85), channel_id=1, source_target_pairs={{16,0},{32,16},{48,32},{64,48},{80,64},{96,80},{112,96},{17,1},{33... | collective-permute-start | bytes 393224 | tf_op jit(solution)/shard_map/ppermute | solution.py:19
  192.6 43.6 %all-to-all-start = ((f16[128,40,128]{2,1,0:T(8,128)(2,1)}), f16[128,40,128]{2,1,0:T(8,128)(2,1)S(1)}, u32[]{:S(2)}, u32[]{:S(2)}) async-start(f16[128,40,128]{2,1,0:T(8,128)(2,1)} %maximum_maximum_fusion.2), calls=%async_computation | async-start | bytes 2621440 | tf_op jit(solution)/shard_map/all_to_all | solution.py:142
  206.4 17.1 %collective-permute-start.26 = (bf16[256,18,1]{0,2,1:T(2,128)(2,1)S(1)}, bf16[256,18,1]{0,2,1:T(2,128)(2,1)S(1)}, u32[]{:S(2)}, u32[]{:S(2)}) collective-permute-start(bf16[256,18,1]{0,2,1:T(2,128)(2,1)S(1)} %get-tuple-element.76), channel_id=1, source_target_pairs={{1,0},{2,1},{3,2},{4,3},{5,4},{6,5},{7,6},{8,7},{9,8},{10,9},{11,1... | collective-permute-start | bytes 27656 | tf_op jit(solution)/shard_map/ppermute | solution.py:19
  209.4 14.1 %collective-permute-start.27 = (bf16[256,18,1]{0,2,1:T(2,128)(2,1)S(1)}, bf16[256,18,1]{0,2,1:T(2,128)(2,1)S(1)}, u32[]{:S(2)}, u32[]{:S(2)}) collective-permute-start(bf16[256,18,1]{0,2,1:T(2,128)(2,1)S(1)} %get-tuple-element.77), channel_id=1, source_target_pairs={{0,1},{1,2},{2,3},{3,4},{4,5},{5,6},{6,7},{7,8},{8,9},{9,10},{10,1... | collective-permute-start | bytes 27656 | tf_op jit(solution)/shard_map/ppermute | solution.py:17
  239.6 30.0 %all-to-all-start.1 = ((f16[128,40,128]{2,1,0:T(8,128)(2,1)}), f16[128,40,128]{2,1,0:T(8,128)(2,1)S(1)}, u32[]{:S(2)}, u32[]{:S(2)}) async-start(f16[128,40,128]{2,1,0:T(8,128)(2,1)} %broadcast_in_dim.29), calls=%async_computation.1 | async-start | bytes 2621440 | tf_op jit(solution)/shard_map/all_to_all | solution.py:146
  (29 other events, 409.7 us)
